TPU v7x, 256 devices: a whole 4x4x8 slice. The times are simulated.
256 devices in a mesh: row: 8 (over y, core), col: 32 (over x, z).
Axes of the slice: x: 4, y: 4, z: 8, core: 2. Of those that a mesh axis runs over, the one named last changes fastest.
Arguments:
- kkt: float32 [8192, 8192], P('row', 'col'), may hold values from -4 to 4, as said below
- swaps: int32 [2, 2, 128], replicated, may hold values from 0 to 8191, as said below
- inverses: float32 [2, 256, 256], replicated
- pivots: float32 [2, 256], replicated, may hold values from -0.12 to 0.12
- couplings: float32 [2, 256], replicated, may hold values from -0.12 to 0.12
- pattern: int32 [2, 256], replicated, may hold values from 0 to 1, as said below
Outputs:
- factored: float32 [8192, 8192], P('row', 'col')
Inputs may be any that keep to these rules, and one draw needn't show every extreme that they name: For panel k, swaps[k, 0, :] holds 128 distinct rows among k * 256 to k * 256 + 255, both ends of that range among them, and swaps[k, 1, :] holds 128 distinct rows among (k + 1) * 256 to 8191, both ends of that range among them. pattern[k, i] = 1 makes rows i and i + 1 one 2 x 2 block of D; no two neighbouring entries are both 1 and the last entry is 0. kkt is the stored order of a symmetric matrix.
All inputs are finite; a program needn't handle non-finite values.
Results may differ from a plain program's by a relative error of at most 0.00014.
Values sent between devices are 32-bit elements; how exact they have to be, the bound alone decides.
A program may use at most 64 MiB of HBM per device.

v0:
```python
import jax
import jax.numpy as jnp
from jax import lax
from jax.sharding import Mesh
from jax.sharding import PartitionSpec as P

COL = ("col_0", "col_1")
HI = lax.Precision.HIGHEST


def tdot(a, b):
    return lax.dot_general(
        a, b, (((0,), (0,)), ((), ())), precision=HI, preferred_element_type=jnp.float32
    )


def swapped(rows, lead, partner):
    to_partner = rows[:, None] == lead[None, :]
    to_lead = rows[:, None] == partner[None, :]
    moved = jnp.sum(
        jnp.where(to_partner, partner[None, :], 0) + jnp.where(to_lead, lead[None, :], 0), axis=1
    )
    return jnp.where(jnp.any(to_partner | to_lead, axis=1), moved, rows)


def plan(swaps, tile, row_groups, dtype=jnp.float32):
    width = tile // row_groups
    count = swaps.shape[2]
    partner = swaps[:, 1, :].reshape(-1)
    top = jnp.arange(2 * tile, dtype=jnp.int32)
    rows = jnp.concatenate([top, partner])
    source = swapped(swapped(rows, swaps[1, 0], swaps[1, 1]), swaps[0, 0], swaps[0, 1])
    repeated = jnp.any(swaps[0, 1][:, None] == swaps[1, 1][None, :], axis=1)
    valid = jnp.concatenate([~repeated, jnp.ones((count,), bool)]) & (partner >= 2 * tile)
    sliced = source.reshape(3, row_groups, width).transpose(1, 0, 2)
    return (rows, source, sliced, jnp.where(valid, partner, -1))


def hits(rows, first, tile):
    return (rows[:, None] == first + jnp.arange(tile, dtype=jnp.int32)[None, :]).astype(jnp.float32)


def along_d(lower_t, pivot, coupling, pattern):
    links = coupling * pattern.astype(jnp.float32)
    zero = jnp.zeros((1, lower_t.shape[1]), lower_t.dtype)
    after = jnp.concatenate([lower_t[1:], zero], axis=0)
    before = jnp.concatenate([zero, lower_t[:-1]], axis=0)
    links_before = jnp.concatenate([jnp.zeros((1,), links.dtype), links[:-1]])
    return lower_t * pivot[:, None] + after * links[:, None] + before * links_before[:, None]


def exchange(picked, moves, tile, row_groups, x_size):
    width = tile // row_groups
    row_index = lax.axis_index("row")
    z_index = lax.axis_index("col_1")
    piece = lax.psum_scatter(picked, "row", scatter_dimension=0, tiled=False)
    strip = lax.all_gather(piece, "row")
    mine = lax.psum(jnp.where(z_index == row_index, strip, 0.0), "col_1")
    wide = lax.all_gather(mine, "col_0")
    part = jnp.dot(piece, moves, precision=HI, preferred_element_type=jnp.float32)
    t0, t1, tp = (part[:width], part[width : 2 * width], part[2 * width :])
    corner = jnp.stack(
        [
            t0[:, 2 * tile :],
            t1[:, 2 * tile :],
            tp[:, 2 * tile :],
            t0[:, tile : 2 * tile],
            t0[:, :tile],
            t1[:, tile : 2 * tile],
        ]
    )
    corner = lax.all_gather(lax.psum(corner, COL), "row")
    return (strip, wide, corner)


def shards(kkt, swaps, inverses, pivots, couplings, pattern):
    tile = inverses.shape[1]
    row_groups = lax.axis_size("row")
    x_size = lax.axis_size("col_0")
    z_size = lax.axis_size("col_1")
    row_index = lax.axis_index("row")
    col_index = lax.axis_index(COL)
    rows, source, sliced, partner = plan(swaps, tile, row_groups)
    flat = sliced.reshape(-1)
    owned = flat // tile % row_groups == row_index
    taken = jnp.take(kkt, flat // tile // row_groups * tile + flat % tile, axis=0)
    picked = jnp.where(owned[:, None], taken, 0.0).reshape(row_groups, -1, tile)
    moves = hits(source, col_index * tile, tile).T
    strip, wide, corner = exchange(picked, moves, tile, row_groups, x_size)

    def ordered(piece):
        return piece.reshape(row_groups, 3, -1, tile).transpose(1, 0, 2, 3).reshape(-1, tile)

    corner = corner.transpose(1, 0, 2, 3).reshape(6, tile, tile)
    to_partner = corner[0:3].reshape(3 * tile, tile)
    block_01, block_00, block_11 = (corner[3], corner[4], corner[5])
    tiles = [row_index + row_groups * slot for slot in range(x_size)] + [col_index]
    strips = [ordered(wide[slot]) for slot in range(x_size)] + [ordered(strip)]
    marks = [hits(partner, index * tile, tile) for index in tiles]
    keep = [1.0 - jnp.sum(mark, axis=0) for mark in marks]
    fixed = [
        strips[n] * keep[n][None, :]
        + jnp.dot(to_partner, marks[n], precision=HI, preferred_element_type=jnp.float32)
        for n in range(x_size + 1)
    ]
    upper = [jnp.where(tiles[n] == 1, block_01, fixed[n][:tile]) for n in range(x_size + 1)]
    low0 = [jnp.where(tiles[n] > 0, tdot(inverses[0], upper[n]), 0.0) for n in range(x_size + 1)]
    low0_1 = tdot(inverses[0], block_01)
    scaled0_1 = along_d(low0_1, pivots[0], couplings[0], pattern[0])
    scaled0 = along_d(low0[-1], pivots[0], couplings[0], pattern[0])
    low1 = [
        jnp.where(
            tiles[n] > 1,
            tdot(inverses[1], fixed[n][tile : 2 * tile] - tdot(scaled0_1, low0[n])),
            0.0,
        )
        for n in range(x_size + 1)
    ]
    scaled1 = along_d(low1[-1], pivots[1], couplings[1], pattern[1])
    outs = []
    for n in range(x_size):
        base = kkt[n * tile : (n + 1) * tile] * keep[n][:, None] * keep[-1][None, :]
        base = base + tdot(marks[n], fixed[-1][2 * tile :])
        base = base + tdot(fixed[n][2 * tile :] * keep[n][None, :], marks[-1])
        value = base - tdot(low0[n], scaled0) - tdot(low1[n], scaled1)
        value = jnp.where(tiles[n] == 0, scaled0, value)
        value = jnp.where(tiles[n] == 1, scaled1, value)
        at_0 = jnp.where(tiles[n] == 0, block_00, low0[n].T)
        at_1 = jnp.where(tiles[n] == 0, scaled0_1, low1[n].T)
        at_1 = jnp.where(tiles[n] == 1, block_11 - tdot(low0_1, scaled0_1), at_1)
        value = jnp.where(col_index == 0, at_0, value)
        value = jnp.where(col_index == 1, at_1, value)
        outs.append(value)
    return jnp.concatenate(outs, axis=0)


def solution(mesh):
    z_size = mesh.shape["row"]
    finer = Mesh(mesh.devices.reshape(mesh.shape["row"], -1, z_size), ("row", "col_0", "col_1"))
    in_specs = (P("row", COL), P(), P(), P(), P(), P())
    return jax.shard_map(
        shards, mesh=finer, in_specs=in_specs, out_specs=P("row", COL), check_vma=False
    )
```

profile of v0, /device:TPU:1, one launch (start us, length us, event | category | flops | bytes accessed | tf_op | source)
XLA Modules:
  0.0 369.6 jit_solution(7685777161819229525)
XLA Ops:
  6.5 0.8 slice_bitcast_fusion.9
  7.3 0.7 slice.199
  9.6 3.3 gather_fusion
  12.9 1.2 select_select_fusion
  14.2 35.9 %reduce-scatter.2.cloned.1.call-done = f32[1,96,256]{2,1,0:T(8,128)} async-done(((f32[8,96,256]{2,1,0:T(8,128)}), f32[1,96,256]{2,1,0:T(8,128)}) %reduce-scatter.2.cloned.1.call-update) | async-done | bytes 98320 | tf_op jit(solution)/shard_map/reduce_scatter | solution.py:56
  50.1 1.5 fusion.17
  51.6 0.7 copy-done.4
  52.4 16.4 %all_gather.17 = f32[8,96,256]{2,1,0:T(8,128)S(1)} all-gather(f32[1,96,256]{2,1,0:T(8,128)} %reduce-scatter.2.cloned.1.call-done), channel_id=1, replica_groups=mesh['row'=8,'col_0'=4,'col_1'=8] {'row'}, dimensions={0}, use_global_device_ids=true | all-gather | bytes 884736 | tf_op jit(solution)/shard_map/all_gather | solution.py:57
  68.8 1.0 select_bitcast_fusion
  69.8 124.7 %all-reduce.10.cloned.1.call-done = f32[1,6,32,256]{3,2,1,0:T(8,128)} async-done(((f32[1,6,32,256]{3,2,1,0:T(8,128)}), f32[1,6,32,256]{3,2,1,0:T(8,128)}) %all-reduce.10.cloned.1.call-update) | async-done | bytes 196624 | tf_op jit(solution)/shard_map/psum | solution.py:72
  195.3 73.7 %all-reduce.12.cloned.1.call-done = f32[1,8,96,256]{3,2,1,0:T(8,128)} async-done(((f32[1,8,96,256]{3,2,1,0:T(8,128)}), f32[1,8,96,256]{3,2,1,0:T(8,128)}) %all-reduce.12.cloned.1.call-update) | async-done | bytes 786448 | tf_op jit(solution)/shard_map/psum | solution.py:58
  269.2 31.6 %all-gather.3.cloned.1.call-done = f32[8,6,32,256]{3,2,1,0:T(8,128)} async-done(((f32[1,6,32,256]{3,2,1,0:T(8,128)}), f32[8,6,32,256]{3,2,1,0:T(8,128)}) %all-gather.3.cloned.1.call-update) | async-done | bytes 1572880 | tf_op jit(solution)/shard_map/all_gather | solution.py:72
  300.8 1.5 copy.51
  302.4 0.8 fusion.125
  303.4 0.6 fusion.55
  304.0 0.6 convolution_add_fusion.3
  304.6 0.6 convolution_select_fusion.7
  305.5 0.6 convolution_subtract_fusion.11
  306.1 0.6 fusion.8
  307.3 1.2 convolution_add_fusion.6
  308.5 0.5 convolution_add_fusion.8
  309.0 0.5 convolution_add_fusion.10
  309.5 0.5 convolution_add_fusion.12
  310.0 0.6 convolution_subtract_fusion.13
  310.6 33.6 %all-gather.5.cloned.1.call-done = f32[4,8,96,256]{3,2,1,0:T(8,128)} async-done(((f32[1,8,96,256]{3,2,1,0:T(8,128)}), f32[4,8,96,256]{3,2,1,0:T(8,128)}) %all-gather.5.cloned.1.call-update) | async-done | bytes 3145744 | tf_op jit(solution)/shard_map/all_gather | solution.py:59
  344.2 2.2 fusion.124
  346.5 0.6 convolution_add_fusion.2
  347.2 0.6 convolution_add_fusion.1
  347.9 0.6 convolution_add_fusion
  348.6 0.6 convolution_add_fusion.4
  349.6 0.4 convolution_add_fusion.5
  350.0 0.6 convolution_select_fusion.1
  350.6 0.6 convolution_subtract_fusion.2
  351.2 0.4 convolution_add_fusion.7
  351.7 0.6 convolution_select_fusion.3
  352.3 0.8 convolution_subtract_fusion.5
  353.9 0.4 convolution_add_fusion.9
  354.3 0.6 convolution_select_fusion.5
  354.9 0.6 convolution_subtract_fusion.8
  355.9 0.4 convolution_add_fusion.11
  356.4 0.6 bitcast_select_fusion.3
  357.0 0.6 convolution_subtract_fusion.12
  358.0 0.6 convolution_select_fusion
  358.6 0.6 convolution_select_fusion.2
  359.2 0.6 convolution_select_fusion.4
  359.8 0.6 convolution_select_fusion.8
  360.4 0.4 fusion.16
  362.1 1.0 pad_maximum_fusion
  (83 shorter events, 7.4 us)
Async XLA Ops:
  6.5 43.5 %reduce-scatter.2.cloned.1.call-start = ((), (), s32[]{:S(2)}) async-start(), calls=%async_computation.1 | async-start | bytes 884736 | tf_op jit(solution)/shard_map/reduce_scatter | solution.py:56
  14.1 180.4 %all-reduce.10.cloned.1.call-start = ((), (), s32[]{:S(2)}) async-start(), calls=%async_computation.2 | async-start | bytes 393216 | tf_op jit(solution)/shard_map/psum | solution.py:72
  51.6 0.7 copy-start.4
  52.3 142.9 %copy-start.5 = (s32[2,256]{1,0:T(2,128)S(1)}, s32[2,256]{1,0:T(2,128)}, u32[]{:S(2)}) copy-start(s32[2,256]{1,0:T(2,128)} %param.11) | copy-start | bytes 6148
  52.3 142.9 %copy-start.6 = (f32[2,256]{1,0:T(2,128)S(1)}, f32[2,256]{1,0:T(2,128)}, u32[]{:S(2)}) copy-start(f32[2,256]{1,0:T(2,128)} %param.10) | copy-start | bytes 6148
  52.4 216.6 %all-reduce.12.cloned.1.call-start = ((), (), s32[]{:S(2)}) async-start(), calls=%async_computation.4 | async-start | bytes 1572864 | tf_op jit(solution)/shard_map/psum | solution.py:58
  68.8 200.2 %copy-start.7 = (f32[2,256]{1,0:T(2,128)S(1)}, f32[2,256]{1,0:T(2,128)}, u32[]{:S(2)}) copy-start(f32[2,256]{1,0:T(2,128)} %param.9) | copy-start | bytes 6148
  69.8 231.1 %all-gather.3.cloned.1.call-start = ((), (), s32[]{:S(2)}) async-start(), calls=%async_computation.3 | async-start | bytes 1769472 | tf_op jit(solution)/shard_map/all_gather | solution.py:72
  194.5 149.6 %all-gather.5.cloned.1.call-start = ((), (), s32[]{:S(2)}) async-start(), calls=%async_computation.5 | async-start | bytes 3932160 | tf_op jit(solution)/shard_map/all_gather | solution.py:59
  302.4 1.0 copy-start.1
  306.1 1.2 copy-start
  348.6 1.0 copy-start.2
  354.9 1.5 copy-start.3
Sparse Core Ops, SparseCore 0:
  14.2 35.8 reduce-scatter.1
  53.5 140.9 all-reduce.9
  196.8 72.0 all-reduce.11
  270.6 30.1 all-gather.2
  302.5 41.6 all-gather.4
where the time goes:
time: 370 us
  waiting for transfers between devices  300 us (81%)
  matrix products  22.2 us (6%)
  blocking collectives  16.4 us (4%)
  between operations  13.9 us (4%)
  local copies, waits for them, and re-layouts  11.6 us (3%)
  other arithmetic  5.64 us (2%)
    psum x1, waiting for transfers between devices, exchange(): corner = lax.all_gather(lax.psum(corner, COL), 'row')  125 us
    psum x1, waiting for transfers between devices, exchange(): mine = lax.psum(jnp.where(z_index == row_index, strip, 0.0), 'col_1')  73.7 us
    reduce_scatter x1, waiting for transfers between devices, exchange(): piece = lax.psum_scatter(picked, 'row', scatter_dimension=0, tiled=False)  35.9 us
    all_gather x1, waiting for transfers between devices, exchange(): wide = lax.all_gather(mine, 'col_0')  33.6 us
    all_gather x1, waiting for transfers between devices, exchange(): corner = lax.all_gather(lax.psum(corner, COL), 'row')  31.6 us
    dot_general x33, matrix products, tdot(): lax.dot_general(a, b, (((0,), (0,)), ((), ())), precision=HI, preferred_e...  17.9 us
    all_gather x1, blocking collectives, exchange(): strip = lax.all_gather(piece, 'row')  16.4 us
  transfers between devices with their start and end apart: 5, of which 5 were waited for; matrix products, arithmetic and copies ran while one was open for 3% of the time, Pallas kernels for 0%

commit v1 on v0

--- a/solution.py
+++ b/solution.py
@@ -69,7 +69,7 @@
             t1[:, tile : 2 * tile],
         ]
     )
-    corner = lax.all_gather(lax.psum(corner, COL), "row")
+    corner = lax.all_gather(lax.psum(lax.psum(corner, "col_1"), "col_0"), "row")
     return (strip, wide, corner)
 
 

time: 370 us -> 290 us (0.78)
  waiting for transfers between devices: 300 us -> 220 us
    psum x2, waiting for transfers between devices: 198 us -> 120 us  [exchange(): corner = lax.all_gather(lax.psum(lax.psum(corner, 'col_1'), 'col_0'), 'row')]
where the time goes in v1:
time: 290 us
  waiting for transfers between devices  220 us (76%)
  matrix products  22.2 us (8%)
  blocking collectives  16.4 us (6%)
  between operations  13.9 us (5%)
  local copies, waits for them, and re-layouts  11 us (4%)
  other arithmetic  5.64 us (2%)
    psum x2, waiting for transfers between devices, exchange(): corner = lax.all_gather(lax.psum(lax.psum(corner, 'col_1'), 'col_0'), 'row')  120 us
    reduce_scatter x1, waiting for transfers between devices, exchange(): piece = lax.psum_scatter(picked, 'row', scatter_dimension=0, tiled=False)  35.9 us
    all_gather x1, waiting for transfers between devices, exchange(): wide = lax.all_gather(mine, 'col_0')  33.6 us
    all_gather x1, waiting for transfers between devices, exchange(): corner = lax.all_gather(lax.psum(lax.psum(corner, 'col_1'), 'col_0'), 'row')  30.6 us
    dot_general x33, matrix products, tdot(): lax.dot_general(a, b, (((0,), (0,)), ((), ())), precision=HI, preferred_e...  17.9 us
    all_gather x1, blocking collectives, exchange(): strip = lax.all_gather(piece, 'row')  16.4 us
  transfers between devices with their start and end apart: 5, of which 5 were waited for; matrix products, arithmetic and copies ran while one was open for 3% of the time, Pallas kernels for 0%

profile of v1, /device:TPU:1, one launch (start us, length us, event | category | flops | bytes accessed | tf_op | source)
XLA Modules:
  0.0 289.9 jit_solution(5662673322591076577)
XLA Ops:
  6.5 0.8 slice_bitcast_fusion.9
  7.3 0.7 slice.199
  9.6 3.3 %gather_fusion = f32[768,256]{1,0:T(8,128)S(1)} fusion(f32[1024,256]{1,0:T(8,128)} %param.6, s32[1024]{0:T(1024)S(1)} %pad_clamp_fusion), kind=kCustom, calls=%fused_computation | custom fusion | bytes 1575936 | tf_op jit(solution)/shard_map/jit(_take)/gather | solution.py:86
  12.9 1.2 select_select_fusion
  14.2 35.9 %reduce-scatter.2.cloned.1.call-done = f32[1,96,256]{2,1,0:T(8,128)} async-done(((f32[8,96,256]{2,1,0:T(8,128)}), f32[1,96,256]{2,1,0:T(8,128)}) %reduce-scatter.2.cloned.1.call-update) | async-done | bytes 98320 | tf_op jit(solution)/shard_map/reduce_scatter | solution.py:56
  50.1 1.5 fusion.17
  51.6 16.4 %all_gather.17 = f32[8,96,256]{2,1,0:T(8,128)S(1)} all-gather(f32[1,96,256]{2,1,0:T(8,128)} %reduce-scatter.2.cloned.1.call-done), channel_id=1, replica_groups=mesh['row'=8,'col_0'=4,'col_1'=8] {'row'}, dimensions={0}, use_global_device_ids=true | all-gather | bytes 884736 | tf_op jit(solution)/shard_map/all_gather | solution.py:57
  68.1 1.0 select_bitcast_fusion
  69.1 70.6 %all-reduce.13.cloned.1.call-done = (f32[6,32,256]{2,1,0:T(8,128)}, f32[1,8,96,256]{3,2,1,0:T(8,128)}) async-done(((f32[6,32,256]{2,1,0:T(8,128)}, f32[1,8,96,256]{3,2,1,0:T(8,128)}), (f32[6,32,256]{2,1,0:T(8,128)}, f32[1,8,96,256]{3,2,1,0:T(8,128)})) %all-reduce.13.cloned.1.call-update) | async-done | bytes 983056 | tf_op jit(solution)/shard_map/psum | solution.py:72
  139.7 49.7 %all-reduce.11.cloned.1.call-done = f32[1,6,32,256]{3,2,1,0:T(8,128)} async-done(((f32[1,6,32,256]{3,2,1,0:T(8,128)}), f32[1,6,32,256]{3,2,1,0:T(8,128)}) %all-reduce.11.cloned.1.call-update) | async-done | bytes 196624 | tf_op jit(solution)/shard_map/psum | solution.py:72
  190.5 30.6 %all-gather.3.cloned.1.call-done = f32[8,6,32,256]{3,2,1,0:T(8,128)} async-done(((f32[1,6,32,256]{3,2,1,0:T(8,128)}), f32[8,6,32,256]{3,2,1,0:T(8,128)}) %all-gather.3.cloned.1.call-update) | async-done | bytes 1572880 | tf_op jit(solution)/shard_map/all_gather | solution.py:72
  221.0 1.5 copy.51
  222.7 0.8 fusion.125
  223.6 0.6 fusion.55
  224.2 0.6 convolution_add_fusion.3
  224.8 0.6 convolution_select_fusion.7
  225.7 0.6 convolution_subtract_fusion.11
  226.3 0.6 fusion.8
  227.5 1.2 convolution_add_fusion.6
  228.7 0.5 convolution_add_fusion.8
  229.2 0.5 convolution_add_fusion.10
  229.7 0.5 convolution_add_fusion.12
  230.2 0.6 convolution_subtract_fusion.13
  230.8 33.6 %all-gather.5.cloned.1.call-done = f32[4,8,96,256]{3,2,1,0:T(8,128)} async-done(((f32[1,8,96,256]{3,2,1,0:T(8,128)}), f32[4,8,96,256]{3,2,1,0:T(8,128)}) %all-gather.5.cloned.1.call-update) | async-done | bytes 3145744 | tf_op jit(solution)/shard_map/all_gather | solution.py:59
  264.4 2.2 fusion.124
  266.7 0.6 convolution_add_fusion.2
  267.4 0.6 convolution_add_fusion.1
  268.1 0.6 convolution_add_fusion
  268.8 0.6 convolution_add_fusion.4
  269.8 0.4 convolution_add_fusion.5
  270.2 0.6 convolution_select_fusion.1
  270.8 0.6 convolution_subtract_fusion.2
  271.4 0.4 convolution_add_fusion.7
  271.9 0.6 convolution_select_fusion.3
  272.5 0.8 convolution_subtract_fusion.5
  274.1 0.4 convolution_add_fusion.9
  274.6 0.6 convolution_select_fusion.5
  275.2 0.6 convolution_subtract_fusion.8
  276.2 0.4 convolution_add_fusion.11
  276.6 0.6 bitcast_select_fusion.3
  277.2 0.6 convolution_subtract_fusion.12
  278.2 0.6 convolution_select_fusion
  278.8 0.6 convolution_select_fusion.2
  279.4 0.6 convolution_select_fusion.4
  280.0 0.6 convolution_select_fusion.8
  280.6 0.4 fusion.16
  281.1 0.4 fusion.14
  282.3 1.0 pad_maximum_fusion
  (83 shorter events, 7.0 us)
Async XLA Ops:
  6.5 43.5 %reduce-scatter.2.cloned.1.call-start = ((), (), s32[]{:S(2)}) async-start(), calls=%async_computation.1 | async-start | bytes 884736 | tf_op jit(solution)/shard_map/reduce_scatter | solution.py:56
  14.1 125.5 %all-reduce.13.cloned.1.call-start = ((), (), s32[]{:S(2)}) async-start(), calls=%async_computation.5 | async-start | bytes 1966080 | tf_op jit(solution)/shard_map/psum | solution.py:72
  51.6 17.4 %copy-start.4 = (f32[6,32,256]{2,1,0:T(8,128)}, f32[6,32,256]{2,1,0:T(8,128)S(1)}, u32[]{:S(2)}) copy-start(f32[6,32,256]{2,1,0:T(8,128)S(1)} %fusion.108) | copy-start | bytes 589828
  68.0 122.2 %copy-start.5 = (s32[2,256]{1,0:T(2,128)S(1)}, s32[2,256]{1,0:T(2,128)}, u32[]{:S(2)}) copy-start(s32[2,256]{1,0:T(2,128)} %param.11) | copy-start | bytes 6148
  68.0 122.2 %copy-start.6 = (f32[2,256]{1,0:T(2,128)S(1)}, f32[2,256]{1,0:T(2,128)}, u32[]{:S(2)}) copy-start(f32[2,256]{1,0:T(2,128)} %param.10) | copy-start | bytes 6148
  68.0 122.3 %copy-start.7 = (f32[2,256]{1,0:T(2,128)S(1)}, f32[2,256]{1,0:T(2,128)}, u32[]{:S(2)}) copy-start(f32[2,256]{1,0:T(2,128)} %param.9) | copy-start | bytes 6148
  69.0 120.4 %all-reduce.11.cloned.1.call-start = ((), (), s32[]{:S(2)}) async-start(), calls=%async_computation.2 | async-start | bytes 393216 | tf_op jit(solution)/shard_map/psum | solution.py:72
  139.7 81.4 %all-gather.3.cloned.1.call-start = ((), (), s32[]{:S(2)}) async-start(), calls=%async_computation.3 | async-start | bytes 1769472 | tf_op jit(solution)/shard_map/all_gather | solution.py:72
  189.5 74.9 %all-gather.5.cloned.1.call-start = ((), (), s32[]{:S(2)}) async-start(), calls=%async_computation.4 | async-start | bytes 3932160 | tf_op jit(solution)/shard_map/all_gather | solution.py:59
  222.6 1.0 copy-start.1
  226.3 1.2 copy-start
  268.8 1.0 copy-start.2
  275.2 1.5 copy-start.3
Sparse Core Ops, SparseCore 0:
  14.2 35.8 reduce-scatter.1
  69.2 70.4 all-reduce.12
  142.0 47.4 all-reduce.10
  191.1 29.8 all-gather.2
  222.7 41.6 all-gather.4
